TPU v7x, 256 devices: a whole 4x4x8 slice. The times are simulated.
256 devices in a mesh: rows: 32 (over y, z), rhs: 8 (over x, core).
Axes of the slice: x: 4, y: 4, z: 8, core: 2. Of those that a mesh axis runs over, the one named last changes fastest.
Arguments:
- lower_panels: bfloat16 [131072, 1024], P('rows', 'rhs'), may hold values from -0.03125 to 0.03125
- parent_solution: bfloat16 [131072, 2048], P('rows', 'rhs'), may hold values from -6 to 6
- parent_rows: int32 [131072], P('rows'), may hold values from 0 to 131071, as said below
- live_counts: int32 [32], P('rows'), may hold values from 512 to 4096, as said below
- front_rhs: bfloat16 [1024, 2048], P('rows', 'rhs'), may hold values from -6 to 6
- coupling: float32 [512, 512], replicated, may hold values from -0.25 to 0.25
- inverse_one: float32 [512, 512], replicated, as said below
- inverse_two: float32 [512, 512], replicated, as said below
Outputs:
- solution: float32 [1024, 2048], P('rows', 'rhs')
Inputs may be any that keep to these rules, and one draw needn't show every extreme that they name: `parent_rows`: the 128 entries of an aligned block of one device's 4096 entries all lie among the 4096 rows of one index of rows, the block's owner; two blocks of one device have the same owner exactly when their block numbers differ by a multiple of 32. `live_counts`: the live rows of an index are its first ones. Each count is 4096 divided by 1, 2, 4 or 8, and some index has all 4096. `inverse_one`: upper triangular. `inverse_two`: upper triangular.
All inputs are finite; a program needn't handle non-finite values.
Results may differ from a plain program's by a relative error of at most 0.0003.
Values may be sent and summed in bfloat16 or wider, within the bound.
A program may use at most 64 MiB of HBM per device.

v0:
```python
import jax
import jax.numpy as jnp
from jax import lax
from jax.sharding import PartitionSpec as P

BLK = 128


def left_apply(matrix, right):
    return jnp.dot(
        matrix, right, precision=lax.Precision.HIGHEST, preferred_element_type=jnp.float32
    )


def body(
    lower_panels,
    parent_solution,
    parent_rows,
    live_counts,
    front_rhs,
    coupling,
    inverse_one,
    inverse_two,
):
    groups = lax.axis_size("rows")
    rows_dev = parent_rows.shape[0]
    block_count = rows_dev // BLK
    slot_count = (block_count + groups - 1) // groups
    columns_dev = parent_solution.shape[1]
    panel_width = inverse_one.shape[0]
    pivot_width = 2 * panel_width
    pivot_share = front_rhs.shape[0]
    start_own = lax.axis_index("rows") * pivot_share
    block_lists = parent_rows.reshape(block_count, BLK)
    owners = block_lists[:, 0] // rows_dev
    local_rows = block_lists - owners[:, None] * rows_dev
    slot_of = jnp.arange(block_count, dtype=jnp.int32) // groups
    requests = jnp.zeros((groups, slot_count, BLK), jnp.int32).at[owners, slot_of].set(local_rows)
    received = lax.all_to_all(requests, "rows", split_axis=0, concat_axis=0, tiled=True)
    picked = parent_solution[received.reshape(-1)].reshape(received.shape + (columns_dev,))
    returned = lax.all_to_all(picked, "rows", split_axis=0, concat_axis=0, tiled=True)
    fetched = returned[owners, slot_of].reshape(rows_dev, columns_dev)
    live_mask = jnp.arange(rows_dev, dtype=jnp.int32) < live_counts[0]
    values = jnp.where(live_mask[:, None], fetched, jnp.zeros((), fetched.dtype))
    rhs_float = front_rhs.astype(jnp.float32)
    placed = lax.dynamic_update_slice(
        jnp.zeros((pivot_width, columns_dev), jnp.float32), rhs_float, (start_own, 0)
    )
    product = lax.dot_general(
        lax.all_gather(lower_panels, "rhs", axis=1, tiled=True),
        values,
        (((0,), (0,)), ((), ())),
        preferred_element_type=jnp.float32,
    )
    shares = lax.psum_scatter(placed - product, "rows", scatter_dimension=0, tiled=True)
    residual = lax.all_gather(shares, "rows", axis=0, tiled=True)
    second = left_apply(inverse_two, residual[panel_width:])
    reduced = residual[:panel_width] - left_apply(coupling, second)
    first = left_apply(inverse_one, reduced)
    solved = jnp.concatenate([first, second], axis=0)
    return lax.dynamic_slice_in_dim(solved, start_own, pivot_share, 0)


def solution(mesh):
    return jax.shard_map(
        body,
        mesh=mesh,
        in_specs=(
            P("rows", "rhs"),
            P("rows", "rhs"),
            P("rows"),
            P("rows"),
            P("rows", "rhs"),
            P(),
            P(),
            P(),
        ),
        out_specs=P("rows", "rhs"),
        check_vma=False,
    )
```

profile of v0, /device:TPU:2, one launch (start us, length us, event | category | flops | bytes accessed | tf_op | source)
XLA Modules:
  0.0 423.7 jit_solution(2627903179569624096)
XLA Ops:
  6.5 0.0 copy-start
  6.5 0.0 all-gather.3.cloned.1.call-start
  6.5 0.7 all-gather.3.cloned.1.call-update
  7.3 0.9 fusion.14
  8.1 0.9 scatter_custom_fusion
  9.1 21.1 %all_to_all.10 = s32[32,1,128]{2,1,0:T(1,128)S(1)} all-to-all(s32[32,1,128]{2,1,0:T(1,128)S(1)} %bitcast.40), channel_id=1, replica_groups=mesh['rows'=32,'rhs'=8] {'rows'}, dimensions={0} | all-to-all | bytes 32768 | tf_op jit(solution)/shard_map/all_to_all | solution.py:39
  30.2 0.0 copy-done
  30.2 17.0 %gather_fusion = bf16[4096,256]{1,0:T(8,128)(2,1)} fusion(bf16[4096,256]{1,0:T(8,128)(2,1)S(1)} %copy-done, s32[4096]{0:T(1024)S(1)} %broadcast_clamp_fusion), kind=kCustom, calls=%fused_computation | custom fusion | bytes 4210688 | tf_op jit(solution)/shard_map/gather | solution.py:40
  47.3 0.0 copy-start.3
  47.3 4.9 %all-to-all-start.1 = ((bf16[32,1,128,256]{3,2,1,0:T(8,128)(2,1)}), bf16[32,1,128,256]{3,2,1,0:T(8,128)(2,1)}, u32[]{:S(2)}, u32[]{:S(2)}) async-start(bf16[32,1,128,256]{3,2,1,0:T(8,128)(2,1)} %bitcast.37), calls=%async_computation.1 | async-start | bytes 4194304 | tf_op jit(solution)/shard_map/all_to_all | solution.py:41
  52.2 0.0 reduce-scatter.4.cloned.1.call-start
  52.2 0.0 copy-done.3
  52.2 0.1 copy.21
  53.0 0.1 broadcast_in_dim.12
  53.1 1.1 dynamic_update_slice.3
  54.2 47.0 %all-to-all-done.1 = bf16[32,1,128,256]{3,2,1,0:T(8,128)(2,1)} async-done(((bf16[32,1,128,256]{3,2,1,0:T(8,128)(2,1)}), bf16[32,1,128,256]{3,2,1,0:T(8,128)(2,1)}, u32[]{:S(2)}, u32[]{:S(2)}) %all-to-all-start.1) | async-done | bytes 2097184 | tf_op jit(solution)/shard_map/all_to_all | solution.py:41
  101.3 3.6 gather_fusion.1
  104.8 2.9 bitcast_select_fusion
  107.8 0.0 all-gather.3.cloned.1.call-done
  107.8 7.4 %fusion = f32[1024,256]{0,1:T(8,128)} fusion(f32[1024,256]{0,1:T(8,128)S(1)} %dynamic_update_slice.3, bf16[4096,256]{1,0:T(8,128)(2,1)} %bitcast_select_fusion, bf16[4096,1024]{1,0:T(8,128)(2,1)} %all-gather.3.cloned.1.call-done), kind=kOutput, calls=%fused_computation.5 | convolution fusion | flops 2147745792 | bytes 12582912 | tf_op jit(solution)/shard_map/dot_general | solution.py:49
  115.1 2.5 copy.27
  117.7 0.0 reduce-scatter.4.cloned.1.call-update
  117.7 0.0 all-gather.5.cloned.1.call-start
  117.7 214.4 %reduce-scatter.4.cloned.1.call-done = f32[32,256]{1,0:T(8,128)} async-done(((f32[1024,256]{1,0:T(8,128)}), f32[32,256]{1,0:T(8,128)}) %reduce-scatter.4.cloned.1.call-update) | async-done | bytes 32784 | tf_op jit(solution)/shard_map/reduce_scatter | solution.py:55
  332.2 0.0 all-gather.5.cloned.1.call-update
  332.2 77.3 %all-gather.5.cloned.1.call-done = f32[1024,256]{1,0:T(8,128)} async-done(((f32[32,256]{1,0:T(8,128)}), f32[1024,256]{1,0:T(8,128)}) %all-gather.5.cloned.1.call-update) | async-done | bytes 1048592 | tf_op jit(solution)/shard_map/all_gather | solution.py:56
  409.5 1.1 slice.19
  410.6 0.2 copy.29
  410.8 0.0 copy-start.1
  410.8 0.0 copy-start.2
  410.8 3.4 fusion.2
  414.2 0.0 copy-done.1
  414.2 1.1 fusion.1
  415.3 0.0 copy-done.2
  415.3 1.1 convolution_bitcast_fusion.1
  416.3 0.1 fusion.4
  416.5 0.7 copy.26
  (3 shorter events, 0.0 us)
Async XLA Ops:
  6.5 23.7 %copy-start = (bf16[4096,256]{1,0:T(8,128)(2,1)S(1)}, bf16[4096,256]{1,0:T(8,128)(2,1)}, u32[]{:S(2)}) copy-start(bf16[4096,256]{1,0:T(8,128)(2,1)} %param.9) | copy-start | bytes 6291460
  6.5 101.2 %all-gather.3.cloned.1.call-start = ((), (), s32[]{:S(2)}) async-start(), calls=%async_computation.3 | async-start | bytes 9437184 | tf_op jit(solution)/shard_map/all_gather | solution.py:50
  47.3 5.0 %copy-start.3 = (bf16[32,256]{1,0:T(8,128)(2,1)S(1)}, bf16[32,256]{1,0:T(8,128)(2,1)}, u32[]{:S(2)}) copy-start(bf16[32,256]{1,0:T(8,128)(2,1)} %param.12) | copy-start | bytes 49156
  47.3 54.0 %all-to-all-start.1 = ((bf16[32,1,128,256]{3,2,1,0:T(8,128)(2,1)}), bf16[32,1,128,256]{3,2,1,0:T(8,128)(2,1)}, u32[]{:S(2)}, u32[]{:S(2)}) async-start(bf16[32,1,128,256]{3,2,1,0:T(8,128)(2,1)} %bitcast.37), calls=%async_computation.1 | async-start | bytes 4194304 | tf_op jit(solution)/shard_map/all_to_all | solution.py:41
  52.2 280.0 %reduce-scatter.4.cloned.1.call-start = ((), (), s32[]{:S(2)}) async-start(), calls=%async_computation.5 | async-start | bytes 1081344 | tf_op jit(solution)/shard_map/reduce_scatter | solution.py:55
  117.7 291.8 %all-gather.5.cloned.1.call-start = ((), (), s32[]{:S(2)}) async-start(), calls=%async_computation.4 | async-start | bytes 1081344 | tf_op jit(solution)/shard_map/all_gather | solution.py:56
  410.8 3.4 copy-start.1
  410.8 4.5 %copy-start.2 = (f32[512,512]{1,0:T(8,128)S(1)}, f32[512,512]{1,0:T(8,128)}, u32[]{:S(2)}) copy-start(f32[512,512]{1,0:T(8,128)} %param.14) | copy-start | bytes 3145732
Sparse Core Ops, SparseCore 0:
  9.2 58.8 all-gather.2
  117.8 214.3 reduce-scatter.3
  334.8 74.6 all-gather.4
where the time goes:
time: 424 us
  waiting for transfers between devices  340 us (80%)
  local copies, waits for them, and re-layouts  26.4 us (6%)
  blocking collectives  21.1 us (5%)
  between operations  13.9 us (3%)
  matrix products  12.8 us (3%)
  starting transfers between devices  4.99 us (1%)
  other arithmetic  4.92 us (1%)
    reduce_scatter x1, waiting for transfers between devices, body(): lax.psum_scatter(placed - product, 'rows', scatter_dimension=0, tiled=True)  214 us
    all_gather x1, waiting for transfers between devices, body(): residual = lax.all_gather(shares, 'rows', axis=0, tiled=True)  77.3 us
    all_to_all x1, waiting for transfers between devices, body(): lax.all_to_all(picked, 'rows', split_axis=0, concat_axis=0, tiled=True)  47 us
    all_to_all x1, blocking collectives, body(): lax.all_to_all(requests, 'rows', split_axis=0, concat_axis=0, tiled=True)  21.1 us
    gather x1, local copies, waits for them, and re-layouts, body(): parent_solution[received.reshape(-1)]  17 us
  transfers between devices with their start and end apart: 4, of which 3 were waited for; matrix products, arithmetic and copies ran while one was open for 6% of the time, Pallas kernels for 0%

commit v1 on v0

--- a/solution.py
+++ b/solution.py
@@ -53,7 +53,9 @@
         preferred_element_type=jnp.float32,
     )
     shares = lax.psum_scatter(placed - product, "rows", scatter_dimension=0, tiled=True)
-    residual = lax.all_gather(shares, "rows", axis=0, tiled=True)
+    residual = jnp.concatenate(
+        lax.all_to_all(jnp.stack([shares] * lax.axis_size("rows")), "rows", 0, 0), axis=0
+    )
     second = left_apply(inverse_two, residual[panel_width:])
     reduced = residual[:panel_width] - left_apply(coupling, second)
     first = left_apply(inverse_one, reduced)

time: 424 us -> 378 us (0.89)
  waiting for transfers between devices: 340 us -> 262 us
  blocking collectives: 21.1 us -> 50.3 us
    all_gather x1 -> x0, waiting for transfers between devices: 77.3 us -> none  [body(): residual = lax.all_gather(shares, 'rows', axis=0, tiled=True)]
    all_to_all x0 -> x1, blocking collectives: none -> 29.2 us  [body(): lax.all_to_all(jnp.stack([shares] * lax.axis_size('rows')), 'rows', 0, 0)]
  transfers between devices with their start and end apart: 4 -> 3, of which waited for: 3 -> 2; matrix products, arithmetic and copies ran while one was open for 6% -> 7% of each run, Pallas kernels for 0% -> 0%
where the time goes in v1:
time: 378 us; the launch traced here: 376 us
  waiting for transfers between devices  262 us (69%)
  blocking collectives  50.3 us (13%)
  local copies, waits for them, and re-layouts  27.1 us (7%)
  between operations  14.2 us (4%)
  matrix products  12.8 us (3%)
  starting transfers between devices  4.95 us (1%)
  other arithmetic  4.94 us (1%)
    reduce_scatter x1, waiting for transfers between devices, body(): lax.psum_scatter(placed - product, 'rows', scatter_dimension=0, tiled=True)  214 us
    all_to_all x1, waiting for transfers between devices, body(): lax.all_to_all(picked, 'rows', split_axis=0, concat_axis=0, tiled=True)  47 us
    all_to_all x1, blocking collectives, body(): lax.all_to_all(jnp.stack([shares] * lax.axis_size('rows')), 'rows', 0, 0)  29.2 us
    all_to_all x1, blocking collectives, body(): lax.all_to_all(requests, 'rows', split_axis=0, concat_axis=0, tiled=True)  21.1 us
    gather x1, local copies, waits for them, and re-layouts, body(): parent_solution[received.reshape(-1)]  17 us
  transfers between devices with their start and end apart: 3, of which 2 were waited for; matrix products, arithmetic and copies ran while one was open for 7% of the time, Pallas kernels for 0%

profile of v1, /device:TPU:2, one launch (start us, length us, event | category | flops | bytes accessed | tf_op | source)
XLA Modules:
  0.0 376.5 jit_solution(11904859440951922738)
XLA Ops:
  6.5 0.0 copy-start
  6.5 0.0 all-gather.2.cloned.1.call-start
  6.5 0.7 all-gather.2.cloned.1.call-update
  7.3 0.9 fusion.12
  8.1 0.9 scatter_custom_fusion
  9.1 21.1 %all_to_all.15 = s32[32,1,128]{2,1,0:T(1,128)S(1)} all-to-all(s32[32,1,128]{2,1,0:T(1,128)S(1)} %bitcast.45), channel_id=1, replica_groups=mesh['rows'=32,'rhs'=8] {'rows'}, dimensions={0} | all-to-all | bytes 32768 | tf_op jit(solution)/shard_map/all_to_all | solution.py:39
  30.2 0.0 copy-done
  30.2 17.0 %gather_fusion = bf16[4096,256]{1,0:T(8,128)(2,1)} fusion(bf16[4096,256]{1,0:T(8,128)(2,1)S(1)} %copy-done, s32[4096]{0:T(1024)S(1)} %broadcast_clamp_fusion), kind=kCustom, calls=%fused_computation | custom fusion | bytes 4210688 | tf_op jit(solution)/shard_map/gather | solution.py:40
  47.2 0.0 copy-start.3
  47.2 4.9 %all-to-all-start.1 = ((bf16[32,1,128,256]{3,2,1,0:T(8,128)(2,1)}), bf16[32,1,128,256]{3,2,1,0:T(8,128)(2,1)}, u32[]{:S(2)}, u32[]{:S(2)}) async-start(bf16[32,1,128,256]{3,2,1,0:T(8,128)(2,1)} %bitcast.40), calls=%async_computation.1 | async-start | bytes 4194304 | tf_op jit(solution)/shard_map/all_to_all | solution.py:41
  52.2 0.0 reduce-scatter.4.cloned.1.call-start
  52.2 0.0 copy-done.3
  52.2 0.1 copy.27
  53.0 0.1 broadcast_in_dim.12
  53.1 1.1 dynamic_update_slice.3
  54.2 47.0 %all-to-all-done.1 = bf16[32,1,128,256]{3,2,1,0:T(8,128)(2,1)} async-done(((bf16[32,1,128,256]{3,2,1,0:T(8,128)(2,1)}), bf16[32,1,128,256]{3,2,1,0:T(8,128)(2,1)}, u32[]{:S(2)}, u32[]{:S(2)}) %all-to-all-start.1) | async-done | bytes 2097184 | tf_op jit(solution)/shard_map/all_to_all | solution.py:41
  101.2 3.6 gather_fusion.1
  104.8 3.0 bitcast_select_fusion
  107.8 0.0 all-gather.2.cloned.1.call-done
  107.8 7.4 %fusion = f32[1024,256]{0,1:T(8,128)} fusion(f32[1024,256]{0,1:T(8,128)S(1)} %dynamic_update_slice.3, bf16[4096,256]{1,0:T(8,128)(2,1)} %bitcast_select_fusion, bf16[4096,1024]{1,0:T(8,128)(2,1)} %all-gather.2.cloned.1.call-done), kind=kOutput, calls=%fused_computation.5 | convolution fusion | flops 2147745792 | bytes 12582912 | tf_op jit(solution)/shard_map/dot_general | solution.py:49
  115.1 2.5 copy.33
  117.7 0.0 reduce-scatter.4.cloned.1.call-update
  117.7 214.4 %reduce-scatter.4.cloned.1.call-done = f32[32,256]{1,0:T(8,128)} async-done(((f32[1024,256]{1,0:T(8,128)}), f32[32,256]{1,0:T(8,128)}) %reduce-scatter.4.cloned.1.call-update) | async-done | bytes 32784 | tf_op jit(solution)/shard_map/reduce_scatter | solution.py:55
  332.1 0.9 stack.2
  333.0 29.2 %all_to_all.16 = f32[32,32,256]{2,1,0:T(8,128)S(1)} all-to-all(f32[32,32,256]{2,1,0:T(8,128)S(1)} %stack.2), channel_id=1, replica_groups=mesh['rows'=32,'rhs'=8] {'rows'}, dimensions={0} | all-to-all | bytes 2097152 | tf_op jit(solution)/shard_map/all_to_all | solution.py:57
  362.2 0.9 fusion.18
  363.0 0.2 copy.31
  363.2 0.0 copy-start.1
  363.3 0.0 copy-start.2
  363.3 3.4 fusion.19
  366.7 0.0 copy-done.1
  366.7 1.1 fusion.1
  367.7 0.0 copy-done.2
  367.7 1.1 convolution_bitcast_fusion.1
  368.8 0.1 fusion.2
  369.0 0.7 copy.32
  (3 shorter events, 0.0 us)
Async XLA Ops:
  6.5 23.7 %copy-start = (bf16[4096,256]{1,0:T(8,128)(2,1)S(1)}, bf16[4096,256]{1,0:T(8,128)(2,1)}, u32[]{:S(2)}) copy-start(bf16[4096,256]{1,0:T(8,128)(2,1)} %param.9) | copy-start | bytes 6291460
  6.5 101.3 %all-gather.2.cloned.1.call-start = ((), (), s32[]{:S(2)}) async-start(), calls=%async_computation.4 | async-start | bytes 9437184 | tf_op jit(solution)/shard_map/all_gather | solution.py:50
  47.2 5.0 %copy-start.3 = (bf16[32,256]{1,0:T(8,128)(2,1)S(1)}, bf16[32,256]{1,0:T(8,128)(2,1)}, u32[]{:S(2)}) copy-start(bf16[32,256]{1,0:T(8,128)(2,1)} %param.12) | copy-start | bytes 49156
  47.2 54.0 %all-to-all-start.1 = ((bf16[32,1,128,256]{3,2,1,0:T(8,128)(2,1)}), bf16[32,1,128,256]{3,2,1,0:T(8,128)(2,1)}, u32[]{:S(2)}, u32[]{:S(2)}) async-start(bf16[32,1,128,256]{3,2,1,0:T(8,128)(2,1)} %bitcast.40), calls=%async_computation.1 | async-start | bytes 4194304 | tf_op jit(solution)/shard_map/all_to_all | solution.py:41
  52.2 280.0 %reduce-scatter.4.cloned.1.call-start = ((), (), s32[]{:S(2)}) async-start(), calls=%async_computation.5 | async-start | bytes 1081344 | tf_op jit(solution)/shard_map/reduce_scatter | solution.py:55
  363.2 3.4 copy-start.1
  363.3 4.5 %copy-start.2 = (f32[512,512]{1,0:T(8,128)S(1)}, f32[512,512]{1,0:T(8,128)}, u32[]{:S(2)}) copy-start(f32[512,512]{1,0:T(8,128)} %param.14) | copy-start | bytes 3145732
Sparse Core Ops, SparseCore 0:
  9.2 58.8 all-gather.1
  117.8 214.2 reduce-scatter.3
